TPU v7x, 32 devices: a whole 2x2x4 slice. The times are simulated.
32 devices in a mesh: gx: 8 (over z, y), gy: 4 (over x, core).
Axes of the slice: x: 2, y: 2, z: 4, core: 2. Of those that a mesh axis runs over, the one named last changes fastest.
Arguments:
- conc_start: float32 [64, 32, 128], P('gx', 'gy'), may hold values from 0.5 to 2
- diffusion: float32 [64, 32, 128], P('gx', 'gy'), may hold values from 0.03 to 0.12
- courant: float32 [64, 32, 128], P('gx', 'gy'), may hold values from 0.05 to 0.25
- uptake: float32 [64, 32, 128], P('gx', 'gy'), may hold values from 0.02 to 0.2
- directions: float32 [32, 64, 32, 128], P(None, 'gx', 'gy'), may hold values from -6 to 6
- sensor_cell: int32 [8, 4, 64], P('gx', 'gy'), may hold values from 0 to 8191
- sensor_step: int32 [8, 4, 64], P('gx', 'gy'), may hold values from 1 to 4
Outputs:
- curvature_product: float32 [32, 64, 32, 128], P(None, 'gx', 'gy')
All inputs are finite; a program needn't handle non-finite values.
Results may differ from a plain program's by a relative error of at most 0.00002.
Values sent between devices are 32-bit elements; how exact they have to be, the bound alone decides.
A program may use at most 64 MiB of HBM per device.

v0:
```python
import jax
import jax.numpy as jnp
from jax import lax
from jax.sharding import PartitionSpec as P

STEPS = 4


HALF_SATURATION = 0.5
PRIOR_WEIGHT = 0.2
PRIOR_SHIFT = 0.5


def padded_2(cells, sides, width):
    for axis, dim in sides:
        count = lax.axis_size(axis)
        ends = count - 1
        head = lax.slice_in_dim(cells, 0, width, axis=dim)
        tail = lax.slice_in_dim(cells, cells.shape[dim] - width, cells.shape[dim], axis=dim)
        cells = jnp.concatenate(
            [
                lax.ppermute(tail, axis, [(i, (i + 1) % count) for i in range(ends)]),
                cells,
                lax.ppermute(head, axis, [((i + 1) % count, i) for i in range(ends)]),
            ],
            axis=dim,
        )
    return cells


def spread(padded):
    inner = padded[..., 1:-1, 1:-1, :]
    column = jnp.pad(inner, [(0, 0)] * (inner.ndim - 1) + [(1, 1)])
    beside = padded[..., 2:, 1:-1, :] + padded[..., :-2, 1:-1, :]
    beside = beside + padded[..., 1:-1, 2:, :] + padded[..., 1:-1, :-2, :]
    beside = beside + column[..., 2:] + column[..., :-2]
    return (inner, beside)


def lifted(field):
    return jnp.pad(field, [(0, 0)] * (field.ndim - 1) + [(1, 0)])[..., :-1]


def dropped(field):
    return jnp.pad(field, [(0, 0)] * (field.ndim - 1) + [(0, 1)])[..., 1:]


def base_step(padded, diffusion, courant, uptake):
    inner, beside = spread(padded)
    carried = courant * inner
    return (
        inner
        + diffusion * (beside - 6.0 * inner)
        + lifted(carried)
        - carried
        - uptake * inner / (HALF_SATURATION + inner)
    )


def tangent_step(padded, diffusion, courant, linear, source):
    inner, beside = spread(padded)
    carried = courant * inner
    return (
        inner
        + diffusion * (beside - 6.0 * inner)
        + lifted(carried)
        - carried
        - linear * inner
        - source
    )


def adjoint_step(padded, adjoint, courant, linear):
    inner_q, beside_q = spread(padded)
    return (
        adjoint
        + beside_q
        - 6.0 * inner_q
        + courant * (dropped(adjoint) - adjoint)
        - linear * adjoint
    )


def read_cells(tangent, cells, when, step):
    values = tangent.reshape(tangent.shape[0], -1)[:, cells]
    return jnp.where(when[None, :] == step, values, jnp.float32(0.0))


def on_device(conc_start, diffusion, courant, uptake, directions, sensor_cell, sensor_step):
    count_dir, size_x, size_y, layers = directions.shape
    cells = sensor_cell.reshape(-1)
    when = sensor_step.reshape(-1)
    observed = []
    states = [conc_start]
    current = conc_start
    for step in range(STEPS):
        padded = padded_2(current, (("gx", 0), ("gy", 1)), 1)
        current = base_step(padded, diffusion, courant, uptake)
        states.append(current)
    ratios = [s / (HALF_SATURATION + s) for s in states[:STEPS]]
    linears = [
        uptake * HALF_SATURATION / ((HALF_SATURATION + s) * (HALF_SATURATION + s))
        for s in states[:STEPS]
    ]
    prior_padded = padded_2(directions, (("gx", 1), ("gy", 2)), 1)
    tangent = -(directions * ratios[0])
    for step in range(1, STEPS + 1):
        if step > 1:
            padded = padded_2(tangent, (("gx", 1), ("gy", 2)), 1)
            tangent = tangent_step(
                padded, diffusion, courant, linears[step - 1], directions * ratios[step - 1]
            )
        observed.append(read_cells(tangent, cells, when, step))
    flat_size = size_x * size_y * layers
    adjoint = jnp.zeros((count_dir, flat_size), jnp.float32).at[:, cells].add(observed[STEPS - 1])
    adjoint = adjoint.reshape(count_dir, size_x, size_y, layers)
    gradient = jnp.zeros((count_dir, size_x, size_y, layers), jnp.float32)
    for step in range(STEPS - 1, -1, -1):
        gradient = gradient - ratios[step] * adjoint
        if step > 0:
            padded = padded_2(diffusion * adjoint, (("gx", 1), ("gy", 2)), 1)
            adjoint = adjoint_step(padded, adjoint, courant, linears[step])
            adjoint = adjoint.reshape(count_dir, flat_size).at[:, cells].add(observed[step - 1])
            adjoint = adjoint.reshape(count_dir, size_x, size_y, layers)
    inner, beside = spread(prior_padded)
    return gradient + PRIOR_WEIGHT * ((6.0 + PRIOR_SHIFT) * inner - beside)


def solution(mesh):
    in_specs = (
        P("gx", "gy", None),
        P("gx", "gy", None),
        P("gx", "gy", None),
        P("gx", "gy", None),
        P(None, "gx", "gy", None),
        P("gx", "gy", None),
        P("gx", "gy", None),
    )
    out_specs = P(None, "gx", "gy", None)
    return jax.shard_map(
        on_device, mesh=mesh, in_specs=in_specs, out_specs=out_specs, check_vma=False
    )
```

profile of v0, /device:TPU:16, one launch (start us, length us, event | category | flops | bytes accessed | tf_op | source)
XLA Modules:
  0.0 244.8 jit_solution(611253817795780404)
XLA Ops:
  15.4 3.7 %collective-permute-start.37 = (f32[32,1,8,128]{3,0,2,1:T(8,128)S(1)}, f32[32,1,8,128]{3,0,2,1:T(8,128)S(1)}, u32[]{:S(2)}, u32[]{:S(2)}) collective-permute-start(f32[32,1,8,128]{3,0,2,1:T(8,128)S(1)} %get-tuple-element.45), channel_id=1, source_target_pairs={{0,4},{4,8},{8,12},{12,16},{16,20},{20,24},{24,28},{1,5},{5,9},{9,... | collective-permute-start | bytes 393224 | tf_op jit(solution)/shard_map/ppermute | solution.py:22
  26.0 3.5 %collective-permute-done.5 = f32[1,8,128]{2,1,0:T(8,128)S(1)} collective-permute-done((f32[1,8,128]{2,1,0:T(8,128)S(1)}, f32[1,8,128]{2,1,0:T(8,128)S(1)}, u32[]{:S(2)}, u32[]{:S(2)}) %collective-permute-start.5) | collective-permute-done | bytes 4128 | tf_op jit(solution)/shard_map/ppermute | solution.py:22
  37.6 3.9 %collective-permute-start.13 = (f32[32,1,8,128]{3,0,2,1:T(8,128)S(1)}, f32[32,1,8,128]{3,0,2,1:T(8,128)S(1)}, u32[]{:S(2)}, u32[]{:S(2)}) collective-permute-start(f32[32,1,8,128]{3,0,2,1:T(8,128)S(1)} %get-tuple-element.41), channel_id=1, source_target_pairs={{0,4},{4,8},{8,12},{12,16},{16,20},{20,24},{24,28},{1,5},{5,9},{9,... | collective-permute-start | bytes 393224 | tf_op jit(solution)/shard_map/ppermute | solution.py:22
  58.8 3.8 %collective-permute-start.16 = (f32[32,1,8,128]{3,0,2,1:T(8,128)S(1)}, f32[32,1,8,128]{3,0,2,1:T(8,128)S(1)}, u32[]{:S(2)}, u32[]{:S(2)}) collective-permute-start(f32[32,1,8,128]{3,0,2,1:T(8,128)S(1)} %get-tuple-element.40), channel_id=1, source_target_pairs={{4,0},{8,4},{12,8},{16,12},{20,16},{24,20},{28,24},{5,1},{9,5},{13... | collective-permute-start | bytes 393224 | tf_op jit(solution)/shard_map/ppermute | solution.py:24
  78.5 4.0 %collective-permute-start.20 = (f32[32,1,8,128]{3,0,2,1:T(8,128)S(1)}, f32[32,1,8,128]{3,0,2,1:T(8,128)S(1)}, u32[]{:S(2)}, u32[]{:S(2)}) collective-permute-start(f32[32,1,8,128]{3,0,2,1:T(8,128)S(1)} %get-tuple-element.38), channel_id=1, source_target_pairs={{4,0},{8,4},{12,8},{16,12},{20,16},{24,20},{28,24},{5,1},{9,5},{13... | collective-permute-start | bytes 393224 | tf_op jit(solution)/shard_map/ppermute | solution.py:24
  85.6 4.7 %collective-permute-done.21 = f32[32,1,8,128]{3,0,2,1:T(8,128)S(1)} collective-permute-done((f32[32,1,8,128]{3,0,2,1:T(8,128)S(1)}, f32[32,1,8,128]{3,0,2,1:T(8,128)S(1)}, u32[]{:S(2)}, u32[]{:S(2)}) %collective-permute-start.21) | collective-permute-done | bytes 131104 | tf_op jit(solution)/shard_map/ppermute | solution.py:22
  91.6 4.1 %collective-permute-start.23 = (f32[32,10,1,128]{3,0,2,1:T(8,128)S(1)}, f32[32,10,1,128]{3,0,2,1:T(8,128)S(1)}, u32[]{:S(2)}, u32[]{:S(2)}) collective-permute-start(f32[32,10,1,128]{3,0,2,1:T(8,128)S(1)} %get-tuple-element.24), channel_id=1, source_target_pairs={{0,1},{1,2},{2,3},{4,5},{5,6},{6,7},{8,9},{9,10},{10,11},{12,13},{... | collective-permute-start | bytes 491528 | tf_op jit(solution)/shard_map/ppermute | solution.py:22
  99.3 3.6 %copy.38 = f32[32,8,8,128]{0,3,2,1:T(8,128)} copy(f32[32,8,8,128]{3,0,2,1:T(8,128)} %fusion.13) | data formatting | bytes 2097152 | tf_op jit(solution)/shard_map/sub | solution.py:64
  103.0 4.2 %scatter_custom_fusion = f32[32,8192]{0,1:T(8,128)} fusion(s32[64]{0:T(128)} %copy-done.22, f32[]{:T(128)} %constant.11.clone.1, pred[64]{0:T(512)(128)(4,1)} %get-tuple-element.67, f32[32,8192]{0,1:T(8,128)} %bitcast.32, s32[1024]{0:T(1024)S(1)} %pad_clamp_fusion), kind=kCustom, calls=%fused_computation.28 | custom fusion | flops 4096 | bytes 2101572 | tf_op jit(solution)/shard_map/scatter-add | solution.py:115
  107.2 3.6 %copy.39 = f32[32,8,8,128]{3,0,2,1:T(8,128)} copy(f32[32,8,8,128]{0,3,2,1:T(8,128)} %bitcast.33) | data formatting | bytes 2097152 | tf_op jit(solution)/shard_map/reshape | solution.py:116
  119.1 3.4 %collective-permute-done.25 = f32[32,1,8,128]{3,0,2,1:T(8,128)S(1)} collective-permute-done((f32[32,1,8,128]{3,0,2,1:T(8,128)S(1)}, f32[32,1,8,128]{3,0,2,1:T(8,128)S(1)}, u32[]{:S(2)}, u32[]{:S(2)}) %collective-permute-start.25) | collective-permute-done | bytes 131104 | tf_op jit(solution)/shard_map/ppermute | solution.py:22
  124.6 6.6 %collective-permute-start.27 = (f32[32,10,1,128]{3,0,2,1:T(8,128)}, f32[32,10,1,128]{3,0,2,1:T(8,128)}, u32[]{:S(2)}, u32[]{:S(2)}) collective-permute-start(f32[32,10,1,128]{3,0,2,1:T(8,128)} %get-tuple-element.22), channel_id=1, source_target_pairs={{0,1},{1,2},{2,3},{4,5},{5,6},{6,7},{8,9},{9,10},{10,11},{12,13},{... | collective-permute-start | bytes 491528 | tf_op jit(solution)/shard_map/ppermute | solution.py:22
  133.8 6.3 %fusion.17 = f32[32,8,8,128]{3,0,2,1:T(8,128)S(1)} fusion(f32[32,8,8,128]{3,0,2,1:T(8,128)} %copy.39, f32[32,8,8,128]{3,0,2,1:T(8,128)} %copy-done.4, f32[32,10,1,128]{3,0,2,1:T(8,128)} %collective-permute-done.27, f32[32,1,8,128]{3,0,2,1:T(8,128)S(1)} %collective-permute-done.24, f32[32,1,8,128]{3,0,2,1:T(8,128)} %copy-done.12, ...), kind=kLoop, calls=%fused_computation.45 | loop fusion | flops 5505024 | bytes 3801088 | tf_op jit(solution)/shard_map/sub | solution.py:76
  142.8 6.2 %scatter_custom_fusion.1 = f32[32,8192]{0,1:T(8,128)} fusion(f32[32,8192]{0,1:T(8,128)} %bitcast.25, s32[64]{0:T(128)} %copy-done.22, f32[]{:T(128)} %constant.11.clone.1, pred[64]{0:T(512)(128)(4,1)S(1)} %get-tuple-element.66, f32[32,8192]{0,1:T(8,128)} %bitcast.30, s32[1024]{0:T(1024)S(1)} %pad_clamp_fusion), kind=kCustom, calls=%fused_computation.263 | custom fusion | flops 4096 | bytes 5247552 | tf_op jit(solution)/shard_map/scatter-add | solution.py:123
  158.9 3.9 %collective-permute-done.29 = f32[32,1,8,128]{3,0,2,1:T(8,128)S(1)} collective-permute-done((f32[32,1,8,128]{3,0,2,1:T(8,128)S(1)}, f32[32,1,8,128]{3,0,2,1:T(8,128)S(1)}, u32[]{:S(2)}, u32[]{:S(2)}) %collective-permute-start.29) | collective-permute-done | bytes 131104 | tf_op jit(solution)/shard_map/ppermute | solution.py:22
  164.9 4.7 %collective-permute-start.31 = (f32[32,10,1,128]{3,0,2,1:T(8,128)}, f32[32,10,1,128]{3,0,2,1:T(8,128)}, u32[]{:S(2)}, u32[]{:S(2)}) collective-permute-start(f32[32,10,1,128]{3,0,2,1:T(8,128)} %get-tuple-element.20), channel_id=1, source_target_pairs={{0,1},{1,2},{2,3},{4,5},{5,6},{6,7},{8,9},{9,10},{10,11},{12,13},{... | collective-permute-start | bytes 491528 | tf_op jit(solution)/shard_map/ppermute | solution.py:22
  175.7 5.5 %fusion.21 = f32[32,8,8,128]{3,0,2,1:T(8,128)S(1)} fusion(f32[32,8,8,128]{3,0,2,1:T(8,128)S(1)} %copy.47, f32[32,8,8,128]{3,0,2,1:T(8,128)} %copy-done.3, f32[32,10,1,128]{3,0,2,1:T(8,128)} %collective-permute-done.31, f32[32,1,8,128]{3,0,2,1:T(8,128)} %copy-done.10, f32[32,1,8,128]{3,0,2,1:T(8,128)} %copy-done.11, ...), kind=kLoop, calls=%fused_computation.49 | loop fusion | flops 5505024 | bytes 3801088 | tf_op jit(solution)/shard_map/sub | solution.py:76
  183.9 6.2 %scatter_custom_fusion.2 = f32[32,8192]{0,1:T(8,128)} fusion(f32[32,8192]{0,1:T(8,128)} %bitcast.27, s32[64]{0:T(128)} %copy-done.22, f32[]{:T(128)} %constant.11.clone.1, pred[64]{0:T(512)(128)(4,1)S(1)} %get-tuple-element.68, f32[32,8192]{0,1:T(8,128)} %bitcast.31, s32[1024]{0:T(1024)S(1)} %pad_clamp_fusion), kind=kCustom, calls=%fused_computation.261 | custom fusion | flops 4096 | bytes 5247552 | tf_op jit(solution)/shard_map/scatter-add | solution.py:123
  196.8 3.9 %collective-permute-start.33 = (f32[32,1,8,128]{3,0,2,1:T(8,128)}, f32[32,1,8,128]{3,0,2,1:T(8,128)}, u32[]{:S(2)}, u32[]{:S(2)}) collective-permute-start(f32[32,1,8,128]{3,0,2,1:T(8,128)} %get-tuple-element.31), channel_id=1, source_target_pairs={{0,4},{4,8},{8,12},{12,16},{16,20},{20,24},{24,28},{1,5},{5,9},{9,... | collective-permute-start | bytes 393224 | tf_op jit(solution)/shard_map/ppermute | solution.py:22
  214.1 5.7 %collective-permute-start.39 = (f32[32,10,1,128]{3,0,2,1:T(8,128)}, f32[32,10,1,128]{3,0,2,1:T(8,128)}, u32[]{:S(2)}, u32[]{:S(2)}) collective-permute-start(f32[32,10,1,128]{3,0,2,1:T(8,128)} %get-tuple-element.30), channel_id=1, source_target_pairs={{0,1},{1,2},{2,3},{4,5},{5,6},{6,7},{8,9},{9,10},{10,11},{12,13},{... | collective-permute-start | bytes 491528 | tf_op jit(solution)/shard_map/ppermute | solution.py:22
  219.7 5.4 %fusion.25 = f32[32,8,8,128]{3,0,2,1:T(8,128)S(1)} fusion(f32[32,8,8,128]{3,0,2,1:T(8,128)S(1)} %copy.55, f32[32,8,8,128]{3,0,2,1:T(8,128)} %copy-done.2, f32[32,10,1,128]{3,0,2,1:T(8,128)S(1)} %collective-permute-done.35, f32[32,1,8,128]{3,0,2,1:T(8,128)} %collective-permute-done.32, f32[32,1,8,128]{3,0,2,1:T(8,128)} %collective-permute-done.33, ...), kind=kLoop, calls=%fused_computation.53 | loop fusion | flops 5505024 | bytes 3801088 | tf_op jit(solution)/shard_map/sub | solution.py:76
  227.9 6.2 %scatter_custom_fusion.3 = f32[32,8192]{0,1:T(8,128)} fusion(f32[32,8192]{0,1:T(8,128)} %bitcast.23, s32[64]{0:T(128)} %copy-done.22, f32[]{:T(128)} %constant.11.clone.1, pred[64]{0:T(512)(128)(4,1)S(1)} %get-tuple-element.65, f32[32,8192]{0,1:T(8,128)} %bitcast.29, s32[1024]{0:T(1024)S(1)} %pad_clamp_fusion), kind=kCustom, calls=%fused_computation.259 | custom fusion | flops 4096 | bytes 5247552 | tf_op jit(solution)/shard_map/scatter-add | solution.py:123
  234.1 3.7 %copy.63 = f32[32,8,8,128]{3,0,2,1:T(8,128)} copy(f32[32,8,8,128]{0,3,2,1:T(8,128)} %bitcast.24) | data formatting | bytes 2097152 | tf_op jit(solution)/shard_map/reshape | solution.py:124
  237.8 5.4 %fusion.57 = f32[32,8,8,128]{3,0,2,1:T(8,128)S(1)} fusion(f32[32,8,8,128]{3,0,2,1:T(8,128)} %copy-done.5, f32[32,10,8,128]{3,0,2,1:T(8,128)} %constant_dynamic-update-slice_fusion.3, f32[32,10,1,128]{3,0,2,1:T(8,128)} %collective-permute-done.39, f32[32,10,1,128]{3,0,2,1:T(8,128)} %collective-permute-done.38, ...), kind=kLoop, calls=%fused_computation.85 | loop fusion | flops 5505024 | bytes 8323072 | tf_op jit(solution)/shard_map/add | solution.py:126
  (164 shorter events, 131.5 us)
Async XLA Ops:
  0.8 8.6 %collective-permute-start.1 = (f32[1,8,128]{2,1,0:T(8,128)S(1)}, f32[1,8,128]{2,1,0:T(8,128)S(1)}, u32[]{:S(2)}, u32[]{:S(2)}) collective-permute-start(f32[1,8,128]{2,1,0:T(8,128)S(1)} %get-tuple-element.64), channel_id=1, source_target_pairs={{0,4},{4,8},{8,12},{12,16},{16,20},{20,24},{24,28},{1,5},{5,9},{9,... | collective-permute-start | bytes 12296 | tf_op jit(solution)/shard_map/ppermute | solution.py:22
  10.3 8.7 %collective-permute-start.2 = (f32[10,1,128]{2,1,0:T(1,128)S(1)}, f32[10,1,128]{2,1,0:T(1,128)S(1)}, u32[]{:S(2)}, u32[]{:S(2)}) collective-permute-start(f32[10,1,128]{2,1,0:T(1,128)S(1)} %get-tuple-element.52), channel_id=1, source_target_pairs={{1,0},{2,1},{3,2},{5,4},{6,5},{7,6},{9,8},{10,9},{11,10},{13,12},{... | collective-permute-start | bytes 15368 | tf_op jit(solution)/shard_map/ppermute | solution.py:24
  15.4 18.6 %collective-permute-start.37 = (f32[32,1,8,128]{3,0,2,1:T(8,128)S(1)}, f32[32,1,8,128]{3,0,2,1:T(8,128)S(1)}, u32[]{:S(2)}, u32[]{:S(2)}) collective-permute-start(f32[32,1,8,128]{3,0,2,1:T(8,128)S(1)} %get-tuple-element.45), channel_id=1, source_target_pairs={{0,4},{4,8},{8,12},{12,16},{16,20},{20,24},{24,28},{1,5},{5,9},{9,... | collective-permute-start | bytes 393224 | tf_op jit(solution)/shard_map/ppermute | solution.py:22
  29.6 11.9 %collective-permute-start.6 = (f32[10,1,128]{2,1,0:T(1,128)S(1)}, f32[10,1,128]{2,1,0:T(1,128)S(1)}, u32[]{:S(2)}, u32[]{:S(2)}) collective-permute-start(f32[10,1,128]{2,1,0:T(1,128)S(1)} %get-tuple-element.50), channel_id=1, source_target_pairs={{1,0},{2,1},{3,2},{5,4},{6,5},{7,6},{9,8},{10,9},{11,10},{13,12},{... | collective-permute-start | bytes 15368 | tf_op jit(solution)/shard_map/ppermute | solution.py:24
  30.9 10.6 %collective-permute-start.7 = (f32[10,1,128]{2,1,0:T(1,128)S(1)}, f32[10,1,128]{2,1,0:T(1,128)S(1)}, u32[]{:S(2)}, u32[]{:S(2)}) collective-permute-start(f32[10,1,128]{2,1,0:T(1,128)S(1)} %get-tuple-element.51), channel_id=1, source_target_pairs={{0,1},{1,2},{2,3},{4,5},{5,6},{6,7},{8,9},{9,10},{10,11},{12,13},{... | collective-permute-start | bytes 15368 | tf_op jit(solution)/shard_map/ppermute | solution.py:22
  37.6 9.0 %collective-permute-start.13 = (f32[32,1,8,128]{3,0,2,1:T(8,128)S(1)}, f32[32,1,8,128]{3,0,2,1:T(8,128)S(1)}, u32[]{:S(2)}, u32[]{:S(2)}) collective-permute-start(f32[32,1,8,128]{3,0,2,1:T(8,128)S(1)} %get-tuple-element.41), channel_id=1, source_target_pairs={{0,4},{4,8},{8,12},{12,16},{16,20},{20,24},{24,28},{1,5},{5,9},{9,... | collective-permute-start | bytes 393224 | tf_op jit(solution)/shard_map/ppermute | solution.py:22
  46.6 10.2 %collective-permute-start.14 = (f32[32,10,1,128]{3,0,2,1:T(8,128)S(1)}, f32[32,10,1,128]{3,0,2,1:T(8,128)S(1)}, u32[]{:S(2)}, u32[]{:S(2)}) collective-permute-start(f32[32,10,1,128]{3,0,2,1:T(8,128)S(1)} %get-tuple-element.27), channel_id=1, source_target_pairs={{1,0},{2,1},{3,2},{5,4},{6,5},{7,6},{9,8},{10,9},{11,10},{13,12},{... | collective-permute-start | bytes 491528 | tf_op jit(solution)/shard_map/ppermute | solution.py:24
  47.9 8.9 %collective-permute-start.15 = (f32[32,10,1,128]{3,0,2,1:T(8,128)S(1)}, f32[32,10,1,128]{3,0,2,1:T(8,128)S(1)}, u32[]{:S(2)}, u32[]{:S(2)}) collective-permute-start(f32[32,10,1,128]{3,0,2,1:T(8,128)S(1)} %get-tuple-element.28), channel_id=1, source_target_pairs={{0,1},{1,2},{2,3},{4,5},{5,6},{6,7},{8,9},{9,10},{10,11},{12,13},{... | collective-permute-start | bytes 491528 | tf_op jit(solution)/shard_map/ppermute | solution.py:22
  51.0 14.3 %collective-permute-start.8 = (f32[1,8,128]{2,1,0:T(8,128)S(1)}, f32[1,8,128]{2,1,0:T(8,128)S(1)}, u32[]{:S(2)}, u32[]{:S(2)}) collective-permute-start(f32[1,8,128]{2,1,0:T(8,128)S(1)} %get-tuple-element.56), channel_id=1, source_target_pairs={{4,0},{8,4},{12,8},{16,12},{20,16},{24,20},{28,24},{5,1},{9,5},{13... | collective-permute-start | bytes 12296 | tf_op jit(solution)/shard_map/ppermute | solution.py:24
  53.9 11.4 %collective-permute-start.9 = (f32[1,8,128]{2,1,0:T(8,128)S(1)}, f32[1,8,128]{2,1,0:T(8,128)S(1)}, u32[]{:S(2)}, u32[]{:S(2)}) collective-permute-start(f32[1,8,128]{2,1,0:T(8,128)S(1)} %get-tuple-element.55), channel_id=1, source_target_pairs={{0,4},{4,8},{8,12},{12,16},{16,20},{20,24},{24,28},{1,5},{5,9},{9,... | collective-permute-start | bytes 12296 | tf_op jit(solution)/shard_map/ppermute | solution.py:22
  58.8 10.8 %collective-permute-start.16 = (f32[32,1,8,128]{3,0,2,1:T(8,128)S(1)}, f32[32,1,8,128]{3,0,2,1:T(8,128)S(1)}, u32[]{:S(2)}, u32[]{:S(2)}) collective-permute-start(f32[32,1,8,128]{3,0,2,1:T(8,128)S(1)} %get-tuple-element.40), channel_id=1, source_target_pairs={{4,0},{8,4},{12,8},{16,12},{20,16},{24,20},{28,24},{5,1},{9,5},{13... | collective-permute-start | bytes 393224 | tf_op jit(solution)/shard_map/ppermute | solution.py:24
  65.3 10.3 %collective-permute-start.10 = (f32[10,1,128]{2,1,0:T(1,128)S(1)}, f32[10,1,128]{2,1,0:T(1,128)S(1)}, u32[]{:S(2)}, u32[]{:S(2)}) collective-permute-start(f32[10,1,128]{2,1,0:T(1,128)S(1)} %get-tuple-element.48), channel_id=1, source_target_pairs={{1,0},{2,1},{3,2},{5,4},{6,5},{7,6},{9,8},{10,9},{11,10},{13,12},{... | collective-permute-start | bytes 15368 | tf_op jit(solution)/shard_map/ppermute | solution.py:24
  66.6 9.0 %collective-permute-start.11 = (f32[10,1,128]{2,1,0:T(1,128)S(1)}, f32[10,1,128]{2,1,0:T(1,128)S(1)}, u32[]{:S(2)}, u32[]{:S(2)}) collective-permute-start(f32[10,1,128]{2,1,0:T(1,128)S(1)} %get-tuple-element.49), channel_id=1, source_target_pairs={{0,1},{1,2},{2,3},{4,5},{5,6},{6,7},{8,9},{9,10},{10,11},{12,13},{... | collective-permute-start | bytes 15368 | tf_op jit(solution)/shard_map/ppermute | solution.py:22
  123.3 10.5 %collective-permute-start.26 = (f32[32,10,1,128]{3,0,2,1:T(8,128)}, f32[32,10,1,128]{3,0,2,1:T(8,128)}, u32[]{:S(2)}, u32[]{:S(2)}) collective-permute-start(f32[32,10,1,128]{3,0,2,1:T(8,128)} %get-tuple-element.21), channel_id=1, source_target_pairs={{1,0},{2,1},{3,2},{5,4},{6,5},{7,6},{9,8},{10,9},{11,10},{13,12},{... | collective-permute-start | bytes 491528 | tf_op jit(solution)/shard_map/ppermute | solution.py:24
  124.6 9.3 %collective-permute-start.27 = (f32[32,10,1,128]{3,0,2,1:T(8,128)}, f32[32,10,1,128]{3,0,2,1:T(8,128)}, u32[]{:S(2)}, u32[]{:S(2)}) collective-permute-start(f32[32,10,1,128]{3,0,2,1:T(8,128)} %get-tuple-element.22), channel_id=1, source_target_pairs={{0,1},{1,2},{2,3},{4,5},{5,6},{6,7},{8,9},{9,10},{10,11},{12,13},{... | collective-permute-start | bytes 491528 | tf_op jit(solution)/shard_map/ppermute | solution.py:22
  163.6 12.1 %collective-permute-start.30 = (f32[32,10,1,128]{3,0,2,1:T(8,128)}, f32[32,10,1,128]{3,0,2,1:T(8,128)}, u32[]{:S(2)}, u32[]{:S(2)}) collective-permute-start(f32[32,10,1,128]{3,0,2,1:T(8,128)} %get-tuple-element.19), channel_id=1, source_target_pairs={{1,0},{2,1},{3,2},{5,4},{6,5},{7,6},{9,8},{10,9},{11,10},{13,12},{... | collective-permute-start | bytes 491528 | tf_op jit(solution)/shard_map/ppermute | solution.py:24
  164.9 10.8 %collective-permute-start.31 = (f32[32,10,1,128]{3,0,2,1:T(8,128)}, f32[32,10,1,128]{3,0,2,1:T(8,128)}, u32[]{:S(2)}, u32[]{:S(2)}) collective-permute-start(f32[32,10,1,128]{3,0,2,1:T(8,128)} %get-tuple-element.20), channel_id=1, source_target_pairs={{0,1},{1,2},{2,3},{4,5},{5,6},{6,7},{8,9},{9,10},{10,11},{12,13},{... | collective-permute-start | bytes 491528 | tf_op jit(solution)/shard_map/ppermute | solution.py:22
  169.7 33.7 %collective-permute-start.36 = (f32[32,1,8,128]{3,0,2,1:T(8,128)}, f32[32,1,8,128]{3,0,2,1:T(8,128)S(1)}, u32[]{:S(2)}, u32[]{:S(2)}) collective-permute-start(f32[32,1,8,128]{3,0,2,1:T(8,128)} %get-tuple-element.44), channel_id=1, source_target_pairs={{4,0},{8,4},{12,8},{16,12},{20,16},{24,20},{28,24},{5,1},{9,5},{13... | collective-permute-start | bytes 393224 | tf_op jit(solution)/shard_map/ppermute | solution.py:24
  194.8 9.2 %collective-permute-start.32 = (f32[32,1,8,128]{3,0,2,1:T(8,128)}, f32[32,1,8,128]{3,0,2,1:T(8,128)}, u32[]{:S(2)}, u32[]{:S(2)}) collective-permute-start(f32[32,1,8,128]{3,0,2,1:T(8,128)} %get-tuple-element.32), channel_id=1, source_target_pairs={{4,0},{8,4},{12,8},{16,12},{20,16},{24,20},{28,24},{5,1},{9,5},{13... | collective-permute-start | bytes 393224 | tf_op jit(solution)/shard_map/ppermute | solution.py:24
  196.8 8.9 %collective-permute-start.33 = (f32[32,1,8,128]{3,0,2,1:T(8,128)}, f32[32,1,8,128]{3,0,2,1:T(8,128)}, u32[]{:S(2)}, u32[]{:S(2)}) collective-permute-start(f32[32,1,8,128]{3,0,2,1:T(8,128)} %get-tuple-element.31), channel_id=1, source_target_pairs={{0,4},{4,8},{8,12},{12,16},{16,20},{20,24},{24,28},{1,5},{5,9},{9,... | collective-permute-start | bytes 393224 | tf_op jit(solution)/shard_map/ppermute | solution.py:22
  206.7 13.0 %collective-permute-start.34 = (f32[32,10,1,128]{3,0,2,1:T(8,128)S(1)}, f32[32,10,1,128]{3,0,2,1:T(8,128)S(1)}, u32[]{:S(2)}, u32[]{:S(2)}) collective-permute-start(f32[32,10,1,128]{3,0,2,1:T(8,128)S(1)} %get-tuple-element.17), channel_id=1, source_target_pairs={{1,0},{2,1},{3,2},{5,4},{6,5},{7,6},{9,8},{10,9},{11,10},{13,12},{... | collective-permute-start | bytes 491528 | tf_op jit(solution)/shard_map/ppermute | solution.py:24
  208.0 11.8 %collective-permute-start.35 = (f32[32,10,1,128]{3,0,2,1:T(8,128)S(1)}, f32[32,10,1,128]{3,0,2,1:T(8,128)S(1)}, u32[]{:S(2)}, u32[]{:S(2)}) collective-permute-start(f32[32,10,1,128]{3,0,2,1:T(8,128)S(1)} %get-tuple-element.18), channel_id=1, source_target_pairs={{0,1},{1,2},{2,3},{4,5},{5,6},{6,7},{8,9},{9,10},{10,11},{12,13},{... | collective-permute-start | bytes 491528 | tf_op jit(solution)/shard_map/ppermute | solution.py:22
  212.8 25.0 %collective-permute-start.38 = (f32[32,10,1,128]{3,0,2,1:T(8,128)}, f32[32,10,1,128]{3,0,2,1:T(8,128)}, u32[]{:S(2)}, u32[]{:S(2)}) collective-permute-start(f32[32,10,1,128]{3,0,2,1:T(8,128)} %get-tuple-element.29), channel_id=1, source_target_pairs={{1,0},{2,1},{3,2},{5,4},{6,5},{7,6},{9,8},{10,9},{11,10},{13,12},{... | collective-permute-start | bytes 491528 | tf_op jit(solution)/shard_map/ppermute | solution.py:24
  214.1 23.7 %collective-permute-start.39 = (f32[32,10,1,128]{3,0,2,1:T(8,128)}, f32[32,10,1,128]{3,0,2,1:T(8,128)}, u32[]{:S(2)}, u32[]{:S(2)}) collective-permute-start(f32[32,10,1,128]{3,0,2,1:T(8,128)} %get-tuple-element.30), channel_id=1, source_target_pairs={{0,1},{1,2},{2,3},{4,5},{5,6},{6,7},{8,9},{9,10},{10,11},{12,13},{... | collective-permute-start | bytes 491528 | tf_op jit(solution)/shard_map/ppermute | solution.py:22
  (40 other events, 547.5 us)
where the time goes:
time: 249 us; the launch traced here: 245 us
  starting transfers between devices  113 us (45%)
  other arithmetic  60.5 us (24%)
  local copies, waits for them, and re-layouts  42.1 us (17%)
  waiting for transfers between devices  28.5 us (11%)
    ppermute x20, starting transfers between devices, padded_2(): lax.ppermute(tail, axis, [(i, (i + 1) % count) for i in range(ends)])  70.5 us
    ppermute x20, starting transfers between devices, padded_2(): lax.ppermute(head, axis, [((i + 1) % count, i) for i in range(ends)])  42.3 us
    ppermute x20, waiting for transfers between devices, padded_2(): lax.ppermute(tail, axis, [(i, (i + 1) % count) for i in range(ends)])  23.4 us
    scatter-add x3, other arithmetic, on_device(): adjoint.reshape(count_dir, flat_size).at[:, cells].add(observed[step - 1])  18.6 us
    sub x3, other arithmetic, adjoint_step(): adjoint + beside_q - 6.0 * inner_q + courant * (dropped(adjoint) - adjoint)  17.2 us
    reshape x4, local copies, waits for them, and re-layouts, on_device(): adjoint = adjoint.reshape(count_dir, size_x, size_y, layers)  12.9 us
    sub x3, local copies, waits for them, and re-layouts, tangent_step(): inner + diffusion * (beside - 6.0 * inner) + lifted(carried) - carried  9.02 us
    sub x3, local copies, waits for them, and re-layouts, adjoint_step(): adjoint + beside_q - 6.0 * inner_q + courant * (dropped(adjoint) - adjoint)  8.17 us
  transfers between devices with their start and end apart: 40, of which 13 were waited for; matrix products, arithmetic and copies ran while one was open for 23% of the time, Pallas kernels for 0%

commit v1 on v0

v1 whole, which is shorter than its diff:
```python
import functools

import jax
import jax.numpy as jnp
from jax import lax
from jax.experimental import pallas as pl
from jax.experimental.pallas import tpu as pltpu
from jax.sharding import PartitionSpec as P

STEPS = 4
HALF_SATURATION = 0.5
PRIOR_WEIGHT = 0.2
PRIOR_SHIFT = 0.5
CHUNKS = 2

MESH = pl.DeviceIdType.MESH


def kernel(
    size_x, size_y, groups, depth,
    conc, diffusion, courant, uptake, dirs, cells, when, out,
    vp, t1, t2, t3, q4, q3, q2, a4, a3, a2,
    cbuf, cface, chx, chy,
    d_s, dz_s, b_s, dl_s, dc_s, a_s, r_s, n_s, r0x, r0y,
    c_send, c_recv, f_send, f_recv,
):
    layers = conc.shape[-1]
    ix, iy = lax.axis_index("gx"), lax.axis_index("gy")
    nx, ny = lax.axis_size("gx"), lax.axis_size("gy")
    have = (ix > 0, ix < nx - 1, iy > 0, iy < ny - 1)
    partner = (
        (jnp.maximum(ix - 1, 0), iy),
        (jnp.minimum(ix + 1, nx - 1), iy),
        (ix, jnp.maximum(iy - 1, 0)),
        (ix, jnp.minimum(iy + 1, ny - 1)),
    )
    barrier = pltpu.get_barrier_semaphore()
    for side in range(4):
        @pl.when(have[side])
        def _(side=side):
            pl.semaphore_signal(barrier, inc=1, device_id=partner[side], device_id_type=MESH)

    padded = (vp, t2, t3, q4, q3, q2)

    def halo(buf, g, side):
        if side == 0:
            return buf.at[g, 0, pl.ds(1, size_y)]
        if side == 1:
            return buf.at[g, size_x + 1, pl.ds(1, size_y)]
        if side == 2:
            return buf.at[g, pl.ds(1, size_x), 0]
        return buf.at[g, pl.ds(1, size_x), size_y + 1]

    def face(buf, g, side):
        if side == 0:
            return buf.at[g, 1, pl.ds(1, size_y)]
        if side == 1:
            return buf.at[g, size_x, pl.ds(1, size_y)]
        if side == 2:
            return buf.at[g, pl.ds(1, size_x), 1]
        return buf.at[g, pl.ds(1, size_x), size_y]

    for side in range(4):
        @pl.when(jnp.logical_not(have[side]))
        def _(side=side):
            for step in range(STEPS - 1):
                chx_or_y = chx if side < 2 else chy
                chx_or_y[step, side % 2] = jnp.zeros(chx.shape[2:] if side < 2 else chy.shape[2:], jnp.float32)
            for buf in padded:
                for g in range(groups):
                    ref = halo(buf, g, side)
                    ref[...] = jnp.zeros(ref.shape, jnp.float32)

    @pl.loop(0, size_x)
    def _(x):
        for y in range(size_y):
            for g in range(groups):
                vp[g, x + 1, y + 1] = dirs[
                    pl.ds(g * depth * size_x * size_y + x * size_y + y, depth, stride=size_x * size_y), :
                ]

    c0 = conc[...]
    cbuf[0] = c0

    def rows_of(c, y):
        return jnp.concatenate([c[x, y:y + 1, :] for x in range(size_x)], axis=0)

    cface[0, 0] = rows_of(c0, 0)
    cface[0, 1] = rows_of(c0, size_y - 1)

    pl.semaphore_wait(barrier, sum(jnp.where(side, 1, 0) for side in have))

    def c_copy(step, side):
        other = side ^ 1
        if side < 2:
            src = cbuf.at[step, 0 if side == 0 else size_x - 1]
            dst = chx.at[step, other]
        else:
            src = cface.at[step, side - 2]
            dst = chy.at[step, other - 2]
        return pltpu.make_async_remote_copy(
            src_ref=src, dst_ref=dst, send_sem=c_send.at[step, side], recv_sem=c_recv.at[step, other],
            device_id=partner[side], device_id_type=MESH,
        )

    def c_landed(step, side):
        dst = chx.at[step, side] if side < 2 else chy.at[step, side - 2]
        return pltpu.make_async_remote_copy(
            src_ref=dst, dst_ref=dst, send_sem=c_send.at[step, side], recv_sem=c_recv.at[step, side],
            device_id=partner[side], device_id_type=MESH,
        )

    def f_copy(k, g, side):
        other = side ^ 1
        return pltpu.make_async_remote_copy(
            src_ref=face(padded[k], g, side), dst_ref=halo(padded[k], g, other),
            send_sem=f_send.at[k, g, side], recv_sem=f_recv.at[k, g, other],
            device_id=partner[side], device_id_type=MESH,
        )

    def f_landed(k, g, side):
        dst = halo(padded[k], g, side)
        return pltpu.make_async_remote_copy(
            src_ref=dst, dst_ref=dst, send_sem=f_send.at[k, g, side], recv_sem=f_recv.at[k, g, side],
            device_id=partner[side], device_id_type=MESH,
        )

    def on_sides(action):
        for side in range(4):
            @pl.when(have[side])
            def _(side=side):
                action(side)

    on_sides(lambda side: c_copy(0, side).start())
    for g in range(groups):
        on_sides(lambda side, g=g: f_copy(0, g, side).start())

    layer = lax.broadcasted_iota(jnp.int32, (size_x, size_y, layers), 2)
    first, last = layer == 0, layer == layers - 1
    zero = jnp.zeros((size_x, size_y, layers), jnp.float32)
    d, u, w = diffusion[...], courant[...], uptake[...]

    def lift(f):
        return jnp.where(first, zero, pltpu.roll(f, 1, 2))

    def drop(f):
        return jnp.where(last, zero, pltpu.roll(f, layers - 1, 2))

    d_s[...] = d
    dz_s[...] = jnp.where(last, zero, d)
    b_s[...] = jnp.where(first, zero, d) + lift(u)
    dl_s[...] = lift(d)
    dc_s[...] = drop(d) + jnp.where(last, zero, u)
    r_s[0] = c0 / (HALF_SATURATION + c0)

    cell, time = cells[...], when[...]
    sensors = cell.shape[1]
    column = lax.broadcasted_iota(jnp.int32, (size_x * size_y, sensors), 0)
    depth_of = lax.broadcasted_iota(jnp.int32, (layers, sensors), 0)
    at_layer = jnp.where((cell % layers) == depth_of, jnp.float32(1), jnp.float32(0))
    for step in range(STEPS):
        at_column = jnp.where(
            ((cell // layers) == column) & (time == step + 1), jnp.float32(1), jnp.float32(0)
        )
        n_s[step] = lax.dot_general(
            at_column, at_layer, (((1,), (1,)), ((), ())), preferred_element_type=jnp.float32
        ).reshape(size_x, size_y, layers)

    def next_conc(step):
        on_sides(lambda side: c_landed(step, side).wait_recv())
        c = cbuf[step]
        low_x, high_x = chx[step, 0], chx[step, 1]
        low_y, high_y = chy[step, 0], chy[step, 1]
        xm = jnp.concatenate([low_x[None], c[:-1]], axis=0)
        xp = jnp.concatenate([c[1:], high_x[None]], axis=0)
        row = lax.broadcasted_iota(jnp.int32, (size_x, size_y, layers), 1)
        low_full = jnp.stack([jnp.broadcast_to(low_y[x:x + 1], (size_y, layers)) for x in range(size_x)], axis=0)
        high_full = jnp.stack([jnp.broadcast_to(high_y[x:x + 1], (size_y, layers)) for x in range(size_x)], axis=0)
        ym = jnp.where(row == 0, low_full, pltpu.roll(c, 1, 1))
        yp = jnp.where(row == size_y - 1, high_full, pltpu.roll(c, size_y - 1, 1))
        beside = xm + xp + ym + yp + lift(c) + drop(c)
        carried = u * c
        new = c + d * (beside - 6.0 * c) + lift(carried) - carried - w * c / (HALF_SATURATION + c)
        if step + 1 < STEPS - 1:
            cbuf[step + 1] = new
            cface[step + 1, 0] = rows_of(new, 0)
            cface[step + 1, 1] = rows_of(new, size_y - 1)
            on_sides(lambda side: c_copy(step + 1, side).start())
        held = HALF_SATURATION + new
        r_s[step + 1] = new / held
        a_s[step] = 1.0 - 6.0 * d - u - w * HALF_SATURATION / (held * held)

    def columns(body):
        @pl.loop(0, size_x)
        def _(x):
            for y in range(size_y):
                body(x, y)

    def coef(ref, x, y, *lead):
        return ref[(*lead, x, pl.ds(y, 1), slice(None))]

    def sides_sum(buf, g, x, y):
        return (buf[g, x, y + 1] + buf[g, x + 2, y + 1]) + (buf[g, x + 1, y] + buf[g, x + 1, y + 2])

    def up(f):
        return pltpu.roll(f, 1, 1)

    def down(f):
        return pltpu.roll(f, layers - 1, 1)

    def tangent_at(buf, g, x, y, step):
        p = buf[g, x + 1, y + 1]
        return (
            coef(a_s, x, y, step - 1) * p
            + coef(d_s, x, y) * sides_sum(buf, g, x, y)
            + coef(dz_s, x, y) * down(p)
            + coef(b_s, x, y) * up(p)
            - coef(r_s, x, y, step) * vp[g, x + 1, y + 1]
        )

    def adjoint_at(held, buf, g, x, y, step):
        a = held[g, x, y]
        return (
            coef(a_s, x, y, step - 1) * a
            + sides_sum(buf, g, x, y)
            + coef(dl_s, x, y) * up(a)
            + coef(dc_s, x, y) * down(a)
        )

    for g in range(groups):
        def first_tangent(x, y, g=g):
            t1[g, x + 1, y + 1] = -(vp[g, x + 1, y + 1] * coef(r_s, x, y, 0))
        columns(first_tangent)

    next_conc(0)
    for side in range(2):
        r0x[side] = chx[0, side] / (HALF_SATURATION + chx[0, side])
        r0y[side] = chy[0, side] / (HALF_SATURATION + chy[0, side])

    for g in range(groups):
        on_sides(lambda side, g=g: f_landed(0, g, side).wait_recv())
        for y in range(size_y):
            t1[g, 0, y + 1] = -(vp[g, 0, y + 1] * r0x[0, pl.ds(y, 1), :])
            t1[g, size_x + 1, y + 1] = -(vp[g, size_x + 1, y + 1] * r0x[1, pl.ds(y, 1), :])
        for x in range(size_x):
            t1[g, x + 1, 0] = -(vp[g, x + 1, 0] * r0y[0, pl.ds(x, 1), :])
            t1[g, x + 1, size_y + 1] = -(vp[g, x + 1, size_y + 1] * r0y[1, pl.ds(x, 1), :])

        def second(x, y, g=g):
            t2[g, x + 1, y + 1] = tangent_at(t1, g, x, y, 1)
        columns(second)
        on_sides(lambda side, g=g: f_copy(1, g, side).start())

    next_conc(1)
    for g in range(groups):
        on_sides(lambda side, g=g: f_landed(1, g, side).wait_recv())

        def third(x, y, g=g):
            t3[g, x + 1, y + 1] = tangent_at(t2, g, x, y, 2)
        columns(third)
        on_sides(lambda side, g=g: f_copy(2, g, side).start())

    next_conc(2)
    for g in range(groups):
        on_sides(lambda side, g=g: f_landed(2, g, side).wait_recv())

        def fourth(x, y, g=g):
            a = coef(n_s, x, y, 3) * tangent_at(t3, g, x, y, 3)
            a4[g, x, y] = a
            q4[g, x + 1, y + 1] = coef(d_s, x, y) * a
        columns(fourth)
        on_sides(lambda side, g=g: f_copy(3, g, side).start())

    for g in range(groups):
        on_sides(lambda side, g=g: f_landed(3, g, side).wait_recv())

        def back_three(x, y, g=g):
            a = adjoint_at(a4, q4, g, x, y, 3) + coef(n_s, x, y, 2) * t3[g, x + 1, y + 1]
            a3[g, x, y] = a
            q3[g, x + 1, y + 1] = coef(d_s, x, y) * a
        columns(back_three)
        on_sides(lambda side, g=g: f_copy(4, g, side).start())

    for g in range(groups):
        on_sides(lambda side, g=g: f_landed(4, g, side).wait_recv())

        def back_two(x, y, g=g):
            a = adjoint_at(a3, q3, g, x, y, 2) + coef(n_s, x, y, 1) * t2[g, x + 1, y + 1]
            a2[g, x, y] = a
            q2[g, x + 1, y + 1] = coef(d_s, x, y) * a
        columns(back_two)
        on_sides(lambda side, g=g: f_copy(5, g, side).start())

    lane = lax.broadcasted_iota(jnp.int32, (1, layers), 1)
    not_first = jnp.where(lane == 0, jnp.float32(0), jnp.float32(1))
    not_last = jnp.where(lane == layers - 1, jnp.float32(0), jnp.float32(1))
    for g in range(groups):
        on_sides(lambda side, g=g: f_landed(5, g, side).wait_recv())

        def finish(x, y, g=g):
            a = adjoint_at(a2, q2, g, x, y, 1) + coef(n_s, x, y, 0) * t1[g, x + 1, y + 1]
            gradient = (
                coef(r_s, x, y, 3) * a4[g, x, y]
                + coef(r_s, x, y, 2) * a3[g, x, y]
                + coef(r_s, x, y, 1) * a2[g, x, y]
                + coef(r_s, x, y, 0) * a
            )
            v = vp[g, x + 1, y + 1]
            beside = sides_sum(vp, g, x, y) + not_first * up(v) + not_last * down(v)
            out[
                pl.ds(g * depth * size_x * size_y + x * size_y + y, depth, stride=size_x * size_y), :
            ] = PRIOR_WEIGHT * ((6.0 + PRIOR_SHIFT) * v - beside) - gradient
        columns(finish)

    for step in range(STEPS - 1):
        on_sides(lambda side, step=step: c_copy(step, side).wait_send())
    for k in range(len(padded)):
        for g in range(groups):
            on_sides(lambda side, k=k, g=g: f_copy(k, g, side).wait_send())


def on_device(conc_start, diffusion, courant, uptake, directions, sensor_cell, sensor_step):
    count_dir, size_x, size_y, layers = directions.shape
    groups = CHUNKS
    depth = count_dir // groups
    sensors = sensor_cell.shape[-1]
    vmem = pltpu.VMEM
    pad = vmem((groups, size_x + 2, size_y + 2, depth, layers), jnp.float32)
    own = vmem((groups, size_x, size_y, depth, layers), jnp.float32)
    block = vmem((size_x, size_y, layers), jnp.float32)

    def blocks(n):
        return vmem((n, size_x, size_y, layers), jnp.float32)

    sems = pltpu.SemaphoreType.DMA
    result = pl.pallas_call(
        functools.partial(kernel, size_x, size_y, groups, depth),
        out_shape=jax.ShapeDtypeStruct((count_dir * size_x * size_y, layers), jnp.float32),
        in_specs=[pl.BlockSpec(memory_space=vmem)] * 7,
        out_specs=pl.BlockSpec(memory_space=vmem),
        scratch_shapes=[
            *[pad] * 7,
            *[own] * 3,
            blocks(STEPS - 1),
            vmem((STEPS - 1, 2, size_x, layers), jnp.float32),
            vmem((STEPS - 1, 2, size_y, layers), jnp.float32),
            vmem((STEPS - 1, 2, size_x, layers), jnp.float32),
            *[block] * 5,
            blocks(STEPS - 1),
            blocks(STEPS),
            blocks(STEPS),
            vmem((2, size_y, layers), jnp.float32),
            vmem((2, size_x, layers), jnp.float32),
            sems((STEPS - 1, 4)),
            sems((STEPS - 1, 4)),
            sems((6, groups, 4)),
            sems((6, groups, 4)),
        ],
        compiler_params=pltpu.CompilerParams(collective_id=0, has_side_effects=True),
    )(
        conc_start, diffusion, courant, uptake,
        directions.reshape(count_dir * size_x * size_y, layers),
        sensor_cell.reshape(1, sensors), sensor_step.reshape(1, sensors),
    )
    return result.reshape(count_dir, size_x, size_y, layers)


def solution(mesh):
    in_specs = (
        P("gx", "gy", None),
        P("gx", "gy", None),
        P("gx", "gy", None),
        P("gx", "gy", None),
        P(None, "gx", "gy", None),
        P("gx", "gy", None),
        P("gx", "gy", None),
    )
    out_specs = P(None, "gx", "gy", None)
    return jax.shard_map(
        on_device, mesh=mesh, in_specs=in_specs, out_specs=out_specs, check_vma=False
    )
```

time: 249 us -> 51.5 us (0.21); the launches traced: 245 us -> 51.3 us
  starting transfers between devices: 113 us -> 0 us
  other arithmetic: 60.5 us -> 0 us
  Pallas kernels: 0 us -> 49 us
  local copies, waits for them, and re-layouts: 42.1 us -> 2.31 us
  waiting for transfers between devices: 28.5 us -> 0 us
    ppermute x40 -> x0, starting transfers between devices: 113 us -> none  [the longest x20 70.5 us: padded_2(): lax.ppermute(tail, axis, [(i, (i + 1) % count) for i in range(ends)])]
    pallas_call x0 -> x1, Pallas kernels: none -> 49 us  [on_device(): pl.pallas_call(functools.partial(kernel, size_x, size_y, groups, depth),...]
    ppermute x40 -> x0, waiting for transfers between devices: 28.5 us -> none  [the longest x20 23.4 us: padded_2(): lax.ppermute(tail, axis, [(i, (i + 1) % count) for i in range(ends)])]
    scatter-add x4 -> x0, other arithmetic: 22.8 us -> none  [the longest x3 18.6 us: on_device(): adjoint.reshape(count_dir, flat_size).at[:, cells].add(observed[step - 1])]
    sub x4 -> x0, other arithmetic: 19.8 us -> none  [the longest x3 17.2 us: adjoint_step(): adjoint + beside_q - 6.0 * inner_q + courant * (dropped(adjoint) - adjoint)]
    sub x6 -> x0, local copies, waits for them, and re-layouts: 17.2 us -> none  [the longest x3 9.02 us: tangent_step(): inner + diffusion * (beside - 6.0 * inner) + lifted(carried) - carried]
    reshape x4 -> x0, local copies, waits for them, and re-layouts: 12.9 us -> none  [on_device(): adjoint = adjoint.reshape(count_dir, size_x, size_y, layers)]
    mul x8 -> x0, other arithmetic: 8.29 us -> none  [the longest x3 5.38 us: tangent_step(): carried = courant * inner]
  transfers between devices with their start and end apart: 40 -> 0, of which waited for: 13 -> 0; matrix products, arithmetic and copies ran while one was open for 23% -> 0% of each run, Pallas kernels for 0% -> 0%
where the time goes in v1:
time: 51.5 us; the launch traced here: 51.3 us
  Pallas kernels  49 us (95%)
  local copies, waits for them, and re-layouts  2.31 us (4%)
    pallas_call x1, Pallas kernels, on_device(): pl.pallas_call(functools.partial(kernel, size_x, size_y, groups, depth),...  49 us
    unnamed x1, local copies, waits for them, and re-layouts  2.31 us

profile of v1, /device:TPU:16, one launch (start us, length us, event | category | flops | bytes accessed | tf_op | source)
XLA Modules:
  0.0 51.3 jit_solution(3817939193756129009)
XLA Ops:
  0.0 49.0 %shard_map.73 = f32[2048,128]{1,0:T(8,128)} custom-call(f32[8,8,128]{2,1,0:T(8,128)} %conc.1, f32[8,8,128]{2,1,0:T(8,128)} %diffusion.1, f32[8,8,128]{2,1,0:T(8,128)} %courant.1, f32[8,8,128]{2,1,0:T(8,128)} %uptake.1, f32[2048,128]{1,0:T(8,128)} %bitcast.5, s32[1,64]{1,0:T(1,128)} %bitcast.6, s32[1,64]{1,0:T(1,128)} %bitcast.7), custom_call_target="tpu_custom_call" | custom-call | tf_op jit(solution)/shard_map/pallas_call | solution.py:336
  49.0 2.3 %copy.9 = f32[32,8,8,128]{3,2,1,0:T(8,128)} copy(f32[32,8,8,128]{3,2,1,0:T(8,128)} %bitcast.4) | data formatting | bytes 2097152

commit v2 on v1

--- a/solution.py
+++ b/solution.py
@@ -11,7 +11,8 @@
 HALF_SATURATION = 0.5
 PRIOR_WEIGHT = 0.2
 PRIOR_SHIFT = 0.5
-CHUNKS = 2
+CHUNKS = 4
+NARROW = (2, 3)
 
 MESH = pl.DeviceIdType.MESH
 
@@ -22,7 +23,8 @@
     vp, t1, t2, t3, q4, q3, q2, a4, a3, a2,
     cbuf, cface, chx, chy,
     d_s, dz_s, b_s, dl_s, dc_s, a_s, r_s, n_s, r0x, r0y,
-    c_send, c_recv, f_send, f_recv,
+    u4, info, info_n, zt, es, er,
+    c_send, c_recv, f_send, f_recv, i_send, i_recv, e_send, e_recv,
 ):
     layers = conc.shape[-1]
     ix, iy = lax.axis_index("gx"), lax.axis_index("gy")
@@ -66,7 +68,14 @@
             for step in range(STEPS - 1):
                 chx_or_y = chx if side < 2 else chy
                 chx_or_y[step, side % 2] = jnp.zeros(chx.shape[2:] if side < 2 else chy.shape[2:], jnp.float32)
-            for buf in padded:
+            if side < 2:
+                info_n[side] = jnp.zeros(info_n.shape[1:], jnp.int32)
+                for k in range(2):
+                    for g in range(groups):
+                        er[k, g, side] = jnp.zeros(er.shape[3:], jnp.float32)
+            for k, buf in enumerate(padded):
+                if side < 2 and k in NARROW:
+                    continue
                 for g in range(groups):
                     ref = halo(buf, g, side)
                     ref[...] = jnp.zeros(ref.shape, jnp.float32)
@@ -78,6 +87,14 @@
                 vp[g, x + 1, y + 1] = dirs[
                     pl.ds(g * depth * size_x * size_y + x * size_y + y, depth, stride=size_x * size_y), :
                 ]
+
+    for g in range(groups):
+        for row in (0, size_x + 1):
+            t3[g, row] = jnp.zeros(t3.shape[2:], jnp.float32)
+    sensors = cells.shape[1]
+    info[...] = jnp.full(info.shape, -1, jnp.int32)
+    info[0:1, 0:sensors] = cells[...]
+    info[1:2, 0:sensors] = when[...]
 
     c0 = conc[...]
     cbuf[0] = c0
@@ -125,13 +142,40 @@
             device_id=partner[side], device_id_type=MESH,
         )
 
-    def on_sides(action):
-        for side in range(4):
+    def i_copy(side):
+        return pltpu.make_async_remote_copy(
+            src_ref=info, dst_ref=info_n.at[side ^ 1], send_sem=i_send.at[side], recv_sem=i_recv.at[side ^ 1],
+            device_id=partner[side], device_id_type=MESH,
+        )
+
+    def e_copy(k, g, side):
+        return pltpu.make_async_remote_copy(
+            src_ref=es.at[k, g, side], dst_ref=er.at[k, g, side ^ 1],
+            send_sem=e_send.at[k, g, side], recv_sem=e_recv.at[k, g, side ^ 1],
+            device_id=partner[side], device_id_type=MESH,
+        )
+
+    def e_landed(k, g, side):
+        return pltpu.make_async_remote_copy(
+            src_ref=er.at[k, g, side], dst_ref=er.at[k, g, side],
+            send_sem=e_send.at[k, g, side], recv_sem=e_recv.at[k, g, side],
+            device_id=partner[side], device_id_type=MESH,
+        )
+
+    def i_landed(side):
+        return pltpu.make_async_remote_copy(
+            src_ref=info_n.at[side], dst_ref=info_n.at[side], send_sem=i_send.at[side], recv_sem=i_recv.at[side],
+            device_id=partner[side], device_id_type=MESH,
+        )
+
+    def on_sides(action, sides=(0, 1, 2, 3)):
+        for side in sides:
             @pl.when(have[side])
             def _(side=side):
                 action(side)
 
     on_sides(lambda side: c_copy(0, side).start())
+    on_sides(lambda side: i_copy(side).start(), (0, 1))
     for g in range(groups):
         on_sides(lambda side, g=g: f_copy(0, g, side).start())
 
@@ -153,11 +197,12 @@
     dc_s[...] = drop(d) + jnp.where(last, zero, u)
     r_s[0] = c0 / (HALF_SATURATION + c0)
 
-    cell, time = cells[...], when[...]
-    sensors = cell.shape[1]
+    cell, time = info[0:1], info[1:2]
+    sensors = info.shape[1]
     column = lax.broadcasted_iota(jnp.int32, (size_x * size_y, sensors), 0)
     depth_of = lax.broadcasted_iota(jnp.int32, (layers, sensors), 0)
     at_layer = jnp.where((cell % layers) == depth_of, jnp.float32(1), jnp.float32(0))
+    zt[2] = at_layer
     for step in range(STEPS):
         at_column = jnp.where(
             ((cell // layers) == column) & (time == step + 1), jnp.float32(1), jnp.float32(0)
@@ -165,6 +210,32 @@
         n_s[step] = lax.dot_general(
             at_column, at_layer, (((1,), (1,)), ((), ())), preferred_element_type=jnp.float32
         ).reshape(size_x, size_y, layers)
+
+    def on_face(where, last_face):
+        base = (size_x - 1) * size_y if last_face else 0
+        col = where[0:1] // layers
+        return [
+            jnp.where((col == base + y) & (where[1:2] == STEPS), jnp.float32(1), jnp.float32(0))
+            for y in range(size_y)
+        ]
+
+    def read_face(rows, which, masks):
+        read = lax.dot_general(
+            jnp.concatenate(rows, axis=0), zt[which], (((1,), (0,)), ((), ())),
+            precision=lax.Precision.HIGHEST, preferred_element_type=jnp.float32,
+        )
+        size = rows[0].shape[0]
+        return functools.reduce(
+            lambda p, q: p + q, [read[y * size:(y + 1) * size] * masks[y] for y in range(size_y)]
+        )
+
+    def place_face(values, which, masks):
+        placed = lax.dot_general(
+            jnp.concatenate([values * m for m in masks], axis=0), zt[which], (((1,), (1,)), ((), ())),
+            precision=lax.Precision.HIGHEST, preferred_element_type=jnp.float32,
+        )
+        size = values.shape[0]
+        return [placed[y * size:(y + 1) * size] for y in range(size_y)]
 
     def next_conc(step):
         on_sides(lambda side: c_landed(step, side).wait_recv())
@@ -251,6 +322,17 @@
         columns(second)
         on_sides(lambda side, g=g: f_copy(1, g, side).start())
 
+    on_sides(lambda side: i_landed(side).wait_recv(), (0, 1))
+    for side in range(2):
+        zt[side] = jnp.where((info_n[side, 0:1] % layers) == depth_of, jnp.float32(1), jnp.float32(0))
+    mine = [on_face(info, side == 1) for side in range(2)]
+    theirs = [on_face(info_n.at[side], side == 0) for side in range(2)]
+    edge = (0, size_x - 1)
+    d_at = [
+        read_face([jnp.broadcast_to(coef(d_s, edge[side], y), (8, layers)) for y in range(size_y)], 2, mine[side])[0:1]
+        for side in range(2)
+    ]
+
     next_conc(1)
     for g in range(groups):
         on_sides(lambda side, g=g: f_landed(1, g, side).wait_recv())
@@ -258,21 +340,43 @@
         def third(x, y, g=g):
             t3[g, x + 1, y + 1] = tangent_at(t2, g, x, y, 2)
         columns(third)
-        on_sides(lambda side, g=g: f_copy(2, g, side).start())
+        on_sides(lambda side, g=g: f_copy(2, g, side).start(), (2, 3))
+        for side in range(2):
+            es[0, g, side] = read_face(
+                [t3[g, edge[side] + 1, y + 1] for y in range(size_y)], side, theirs[side]
+            )
+        on_sides(lambda side, g=g: e_copy(0, g, side).start(), (0, 1))
 
     next_conc(2)
     for g in range(groups):
-        on_sides(lambda side, g=g: f_landed(2, g, side).wait_recv())
+        on_sides(lambda side, g=g: f_landed(2, g, side).wait_recv(), (2, 3))
 
         def fourth(x, y, g=g):
-            a = coef(n_s, x, y, 3) * tangent_at(t3, g, x, y, 3)
+            t4 = tangent_at(t3, g, x, y, 3)
+            a = coef(n_s, x, y, 3) * t4
             a4[g, x, y] = a
             q4[g, x + 1, y + 1] = coef(d_s, x, y) * a
+            u4[g, x, y] = coef(d_s, x, y) * t4
         columns(fourth)
-        on_sides(lambda side, g=g: f_copy(3, g, side).start())
-
-    for g in range(groups):
-        on_sides(lambda side, g=g: f_landed(3, g, side).wait_recv())
+        on_sides(lambda side, g=g: e_landed(0, g, side).wait_recv(), (0, 1))
+        for side in range(2):
+            x = edge[side]
+            added = er[0, g, side] * d_at[side]
+            es[1, g, side] = (
+                read_face([u4[g, x, y] for y in range(size_y)], 2, mine[side]) + d_at[side] * added
+            )
+            for y, more in enumerate(place_face(added, 2, mine[side])):
+                a4[g, x, y] = a4[g, x, y] + more
+                q4[g, x + 1, y + 1] = q4[g, x + 1, y + 1] + coef(d_s, x, y) * more
+        on_sides(lambda side, g=g: e_copy(1, g, side).start(), (0, 1))
+        on_sides(lambda side, g=g: f_copy(3, g, side).start(), (2, 3))
+
+    for g in range(groups):
+        on_sides(lambda side, g=g: f_landed(3, g, side).wait_recv(), (2, 3))
+        on_sides(lambda side, g=g: e_landed(1, g, side).wait_recv(), (0, 1))
+        for side in range(2):
+            for y, more in enumerate(place_face(er[1, g, side], side, theirs[side])):
+                q4[g, 0 if side == 0 else size_x + 1, y + 1] = more
 
         def back_three(x, y, g=g):
             a = adjoint_at(a4, q4, g, x, y, 3) + coef(n_s, x, y, 2) * t3[g, x + 1, y + 1]
@@ -307,16 +411,20 @@
             )
             v = vp[g, x + 1, y + 1]
             beside = sides_sum(vp, g, x, y) + not_first * up(v) + not_last * down(v)
-            out[
-                pl.ds(g * depth * size_x * size_y + x * size_y + y, depth, stride=size_x * size_y), :
-            ] = PRIOR_WEIGHT * ((6.0 + PRIOR_SHIFT) * v - beside) - gradient
+            out[x * size_y + y, g * depth:(g + 1) * depth] = PRIOR_WEIGHT * ((6.0 + PRIOR_SHIFT) * v - beside) - gradient
         columns(finish)
 
     for step in range(STEPS - 1):
         on_sides(lambda side, step=step: c_copy(step, side).wait_send())
     for k in range(len(padded)):
         for g in range(groups):
-            on_sides(lambda side, k=k, g=g: f_copy(k, g, side).wait_send())
+            on_sides(
+                lambda side, k=k, g=g: f_copy(k, g, side).wait_send(), (2, 3) if k in NARROW else (0, 1, 2, 3)
+            )
+    on_sides(lambda side: i_copy(side).wait_send(), (0, 1))
+    for k in range(2):
+        for g in range(groups):
+            on_sides(lambda side, k=k, g=g: e_copy(k, g, side).wait_send(), (0, 1))
 
 
 def on_device(conc_start, diffusion, courant, uptake, directions, sensor_cell, sensor_step):
@@ -324,6 +432,7 @@
     groups = CHUNKS
     depth = count_dir // groups
     sensors = sensor_cell.shape[-1]
+    lanes = pl.cdiv(sensors, 128) * 128
     vmem = pltpu.VMEM
     pad = vmem((groups, size_x + 2, size_y + 2, depth, layers), jnp.float32)
     own = vmem((groups, size_x, size_y, depth, layers), jnp.float32)
@@ -335,7 +444,7 @@
     sems = pltpu.SemaphoreType.DMA
     result = pl.pallas_call(
         functools.partial(kernel, size_x, size_y, groups, depth),
-        out_shape=jax.ShapeDtypeStruct((count_dir * size_x * size_y, layers), jnp.float32),
+        out_shape=jax.ShapeDtypeStruct((size_x * size_y, count_dir, layers), jnp.float32),
         in_specs=[pl.BlockSpec(memory_space=vmem)] * 7,
         out_specs=pl.BlockSpec(memory_space=vmem),
         scratch_shapes=[
@@ -351,10 +460,20 @@
             blocks(STEPS),
             vmem((2, size_y, layers), jnp.float32),
             vmem((2, size_x, layers), jnp.float32),
+            own,
+            pltpu.VMEM((8, lanes), jnp.int32),
+            pltpu.VMEM((2, 8, lanes), jnp.int32),
+            vmem((3, layers, lanes), jnp.float32),
+            vmem((2, groups, 2, depth, lanes), jnp.float32),
+            vmem((2, groups, 2, depth, lanes), jnp.float32),
             sems((STEPS - 1, 4)),
             sems((STEPS - 1, 4)),
             sems((6, groups, 4)),
             sems((6, groups, 4)),
+            sems((2,)),
+            sems((2,)),
+            sems((2, groups, 2)),
+            sems((2, groups, 2)),
         ],
         compiler_params=pltpu.CompilerParams(collective_id=0, has_side_effects=True),
     )(
@@ -362,7 +481,7 @@
         directions.reshape(count_dir * size_x * size_y, layers),
         sensor_cell.reshape(1, sensors), sensor_step.reshape(1, sensors),
     )
-    return result.reshape(count_dir, size_x, size_y, layers)
+    return jnp.swapaxes(result, 0, 1).reshape(count_dir, size_x, size_y, layers)
 
 
 def solution(mesh):

time: 51.5 us -> 46.5 us (0.903)
  Pallas kernels: 49 us -> 43.4 us
    pallas_call x1, Pallas kernels: 49 us -> 43.4 us  [on_device(): pl.pallas_call(functools.partial(kernel, size_x, size_y, groups, depth),...]
    reshape x0 -> x1, local copies, waits for them, and re-layouts: none -> 2.81 us  [on_device(): return jnp.swapaxes(result, 0, 1).reshape(count_dir, size_x, size_y, layers)]
    unnamed x1 -> x0, local copies, waits for them, and re-layouts: 2.31 us -> none
where the time goes in v2:
time: 46.5 us; the launch traced here: 46.2 us
  Pallas kernels  43.4 us (93%)
  local copies, waits for them, and re-layouts  2.81 us (6%)
    pallas_call x1, Pallas kernels, on_device(): pl.pallas_call(functools.partial(kernel, size_x, size_y, groups, depth),...  43.4 us
    reshape x1, local copies, waits for them, and re-layouts, on_device(): return jnp.swapaxes(result, 0, 1).reshape(count_dir, size_x, size_y, layers)  2.81 us

profile of v2, /device:TPU:16, one launch (start us, length us, event | category | flops | bytes accessed | tf_op | source)
XLA Modules:
  0.0 46.2 jit_solution(11334674309517536828)
XLA Ops:
  0.0 43.4 %shard_map.73 = f32[64,32,128]{2,1,0:T(8,128)} custom-call(f32[8,8,128]{2,1,0:T(8,128)} %conc.1, f32[8,8,128]{2,1,0:T(8,128)} %diffusion.1, f32[8,8,128]{2,1,0:T(8,128)} %courant.1, f32[8,8,128]{2,1,0:T(8,128)} %uptake.1, f32[2048,128]{1,0:T(8,128)} %bitcast.7, s32[1,64]{1,0:T(1,128)} %bitcast.8, s32[1,64]{1,0:T(1,128)} %bitcast.9), custom_call_target="tpu_custom_call" | custom-call | tf_op jit(solution)/shard_map/pallas_call | solution.py:445
  43.4 2.8 %copy.8 = f32[32,8,8,128]{3,2,1,0:T(8,128)} copy(f32[32,8,8,128]{3,0,2,1:T(8,128)} %bitcast.6) | data formatting | bytes 2097152 | tf_op jit(solution)/shard_map/reshape | solution.py:484

commit v3 on v2

--- a/solution.py
+++ b/solution.py
@@ -262,10 +262,13 @@
         a_s[step] = 1.0 - 6.0 * d - u - w * HALF_SATURATION / (held * held)
 
     def columns(body):
-        @pl.loop(0, size_x)
-        def _(x):
-            for y in range(size_y):
-                body(x, y)
+        unroll = 2 if size_x % 2 == 0 else 1
+
+        @pl.loop(0, size_x // unroll)
+        def _(pair):
+            for part in range(unroll):
+                for y in range(size_y):
+                    body(pair * unroll + part, y)
 
     def coef(ref, x, y, *lead):
         return ref[(*lead, x, pl.ds(y, 1), slice(None))]

time: 46.5 us -> 44 us (0.946)
  Pallas kernels: 43.4 us -> 40.7 us
    pallas_call x1, Pallas kernels: 43.4 us -> 40.7 us  [on_device(): pl.pallas_call(functools.partial(kernel, size_x, size_y, groups, depth),...]
where the time goes in v3:
time: 44 us; the launch traced here: 43.5 us
  Pallas kernels  40.7 us (93%)
  local copies, waits for them, and re-layouts  2.81 us (6%)
    pallas_call x1, Pallas kernels, on_device(): pl.pallas_call(functools.partial(kernel, size_x, size_y, groups, depth),...  40.7 us
    reshape x1, local copies, waits for them, and re-layouts, on_device(): return jnp.swapaxes(result, 0, 1).reshape(count_dir, size_x, size_y, layers)  2.81 us

profile of v3, /device:TPU:16, one launch (start us, length us, event | category | flops | bytes accessed | tf_op | source)
XLA Modules:
  0.0 43.5 jit_solution(2769796315687945978)
XLA Ops:
  0.0 40.7 %shard_map.73 = f32[64,32,128]{2,1,0:T(8,128)} custom-call(f32[8,8,128]{2,1,0:T(8,128)} %conc.1, f32[8,8,128]{2,1,0:T(8,128)} %diffusion.1, f32[8,8,128]{2,1,0:T(8,128)} %courant.1, f32[8,8,128]{2,1,0:T(8,128)} %uptake.1, f32[2048,128]{1,0:T(8,128)} %bitcast.7, s32[1,64]{1,0:T(1,128)} %bitcast.8, s32[1,64]{1,0:T(1,128)} %bitcast.9), custom_call_target="tpu_custom_call" | custom-call | tf_op jit(solution)/shard_map/pallas_call | solution.py:448
  40.7 2.8 %copy.8 = f32[32,8,8,128]{3,2,1,0:T(8,128)} copy(f32[32,8,8,128]{3,0,2,1:T(8,128)} %bitcast.6) | data formatting | bytes 2097152 | tf_op jit(solution)/shard_map/reshape | solution.py:487
